TPU v7x, 32 devices: a whole 2x2x4 slice. The times are simulated.
32 devices in a mesh: col: 8 (over z, x), row: 4 (over y, core).
Axes of the slice: x: 2, y: 2, z: 4, core: 2. Of those that a mesh axis runs over, the one named last changes fastest.
Arguments:
- positions: float32 [3, 131072], P(None, ('col', 'row')), may hold values from -6 to 6
- velocities: float32 [3, 131072], P(None, ('col', 'row')), may hold values from -4 to 4
- masses: float32 [131072], P(('col', 'row')), may hold values from 7.629395e-09 to 7.6293945e-05
- active_index: int32 [2048], P(('col', 'row')), may hold values from 0 to 4095, as said below
- active_count: int32 [32], P(('col', 'row')), may hold values from 1 to 64, as said below
Outputs:
- accel: float32 [3, 2048], P(None, ('col', 'row'))
- jerk: float32 [3, 2048], P(None, ('col', 'row'))
Inputs may be any that keep to these rules, and one draw needn't show every extreme that they name: `active_index`: entries of block b (slots b * 64 to (b + 1) * 64 - 1) index stars of the block of 4096 that block b owns; the entries of one block are distinct. `active_count`: number of used slots of each block, counted from the block's first slot. Some block uses all 64 slots in every draw.
All inputs are finite; a program needn't handle non-finite values.
Results may differ from a plain program's by a relative error of at most 0.0003.
Values sent between devices are 32-bit elements; how exact they have to be, the bound alone decides.
No kernel may reach another device: no remote copies, remote signals or barrier semaphores. Data moves between devices by JAX's collectives and lax.ppermute only.
A program may use at most 64 MiB of HBM per device.

v0:
```python
import functools

import jax
import jax.numpy as jnp
import numpy as np
from jax import lax
from jax.experimental import pallas as pl
from jax.experimental.pallas import tpu as pltpu
from jax.sharding import PartitionSpec as P

AXES = ("col", "row")
SOFTEN = 0.0001
MARK = 8.0
F32 = jnp.float32
BF16 = jnp.bfloat16
TILE = 128
HALF = 64
CH = 16
BLOCK = 256
PAIRS = ((0, 0), (1, 0), (0, 1), (1, 1), (2, 0), (0, 2))
RAW = 8 * len(PAIRS)
DEPTH = 64
NN = (((1,), (0,)), ((), ()))
NT = (((1,), (1,)), ((), ()))


def vmem():
    return pl.BlockSpec(memory_space=pltpu.VMEM)


def hbm():
    return pl.BlockSpec(memory_space=pltpu.HBM)


def pieces(value):
    first = value.astype(BF16).astype(F32)
    rest = value - first
    second = rest.astype(BF16).astype(F32)
    return first, second, (rest - second).astype(BF16).astype(F32)


def prepare_kernel(parts, index_hbm, count_ref, pos_hbm, vel_hbm, send_ref, index_ref, pos_ref, vel_ref, sems):
    slots = index_ref.shape[0]
    copies = [
        pltpu.make_async_copy(pos_hbm, pos_ref, sems.at[0]),
        pltpu.make_async_copy(vel_hbm, vel_ref, sems.at[1]),
        pltpu.make_async_copy(index_hbm, index_ref, sems.at[2]),
    ]
    for copy in copies:
        copy.start()
    for copy in copies:
        copy.wait()
    lane = lax.broadcasted_iota(jnp.int32, (3, 128), 1)
    picked = jnp.zeros((3, 128), F32)
    for slot in range(slots):
        star = index_ref[slot]
        tile = pl.ds(pl.multiple_of((star >> 7) << 7, 128), 128)
        shift = slot - star
        moved = pltpu.roll(pos_ref[:, tile], shift & 127, 1)
        picked = jnp.where(lane == slot, moved, picked)
        moved = pltpu.roll(vel_ref[:, tile], (shift + slots) & 127, 1)
        picked = jnp.where(lane == slot + slots, moved, picked)
    row = lax.broadcasted_iota(jnp.int32, (3, 128), 0)
    count = count_ref[...]
    mark = (row == 0) & (lane == slots - 1) & (count < slots)
    picked = jnp.where(mark, MARK + count.astype(F32), picked)

    def fill(part, carry):
        for k in range(3):
            send_ref[part, :, 128 * k : 128 * k + 128] = picked[k : k + 1]
        return carry

    lax.fori_loop(0, parts, fill, 0, unroll=8)


def pair_kernel(slots, recv_ref, pos_ref, vel_ref, mass_ref, send_ref, count_smem, offset_smem, dot_ref, sum_ref, slot_ref, own_ref, pull_ref, res_ref, sem):
    parts = recv_ref.shape[0]
    width = pos_ref.shape[1]
    copy = pltpu.make_async_copy(recv_ref.at[:, 0, 0:128], count_smem, sem)
    copy.start()

    def star_step(step, carry):
        cols = pl.ds(pl.multiple_of(step * 512, 512), 512)
        pos, vel, mass = pos_ref[:, cols], vel_ref[:, cols], mass_ref[:, cols]
        heavy = 3.0 * mass
        cross = jnp.sum(pos * vel, axis=0, keepdims=True)
        dots = pieces(jnp.concatenate([-heavy * vel, heavy, -heavy * pos, heavy * cross], axis=0))
        for k, (mine, _) in enumerate(PAIRS):
            dot_ref[8 * k : 8 * k + 8, cols] = dots[mine].astype(BF16)
        dot_ref[RAW:DEPTH, cols] = jnp.zeros((DEPTH - RAW, 512), BF16)
        sums = pieces(jnp.concatenate([mass * pos, mass, mass * vel, jnp.zeros_like(mass)], axis=0))
        for k in range(3):
            sum_ref[8 * k : 8 * k + 8, cols] = sums[k].astype(BF16)
        return carry

    lax.fori_loop(0, width // 512, star_step, 0, unroll=4)
    copy.wait()

    lane = lax.broadcasted_iota(jnp.int32, (8, 128), 1)
    row = lax.broadcasted_iota(jnp.int32, (8, 128), 0)

    def gather(part, total):
        offset_smem[part] = total
        raw = [recv_ref[part, :, 128 * k : 128 * k + 128] for k in range(3)]
        raw = jnp.concatenate([*raw, raw[0]], axis=0)
        own = jnp.concatenate([raw, pltpu.roll(raw, 128 - slots, 1)], axis=0)
        tile, start = total >> 7, total & 127
        moved = pltpu.roll(own, start, 1)
        slot_ref[tile] = jnp.where(lane < start, slot_ref[tile], moved)
        slot_ref[tile + 1] = moved
        last = count_smem[part, slots - 1]
        return total + jnp.where(last < MARK, slots, (last - MARK).astype(jnp.int32))

    total = lax.fori_loop(0, parts, gather, 0, unroll=32)

    def lay_out(tile, place, height):
        slot = slot_ref[tile]
        cross = jnp.sum(slot[0:3] * slot[4:7], axis=0, keepdims=True)
        slot = jnp.where(row == 7, 1.0, jnp.where(row == 3, cross, slot))
        split = pieces(slot)
        rows = [split[theirs] for _, theirs in PAIRS] + [slot, jnp.zeros((DEPTH - RAW - 8, TILE), F32)]
        act = jnp.concatenate(rows, axis=0).T[:height]
        for k in range(3):
            own_ref[place, k, :height, :] = jnp.broadcast_to(act[:, RAW + k : RAW + k + 1], (height, 128))
            pull_ref[place, k, :height, :] = jnp.zeros((height, 128), F32)
        return slot, act.astype(BF16)

    def add_pairs(place, height, left):
        sums = jnp.zeros((24, 2 * height), F32)
        for block in range(width // BLOCK):
            cols = slice(block * BLOCK, block * BLOCK + BLOCK)
            dot = lax.dot_general(left, dot_ref[:, cols], NN, preferred_element_type=F32)
            high, low = [], []
            for chunk in range(height // CH):
                part = slice(chunk * CH, chunk * CH + CH)
                own = [own_ref[place, k, part, :] for k in range(3)]
                acc = [pull_ref[place, k, part, :] for k in range(3)]
                highs, lows = [], []
                for half in range(BLOCK // 128):
                    lanes = slice(block * BLOCK + half * 128, block * BLOCK + half * 128 + 128)
                    star = [jnp.broadcast_to(pos_ref[k : k + 1, lanes], (CH, 128)) for k in range(3)]
                    dx = [star[k] - own[k] for k in range(3)]
                    squared = dx[2] * dx[2] + (dx[1] * dx[1] + (dx[0] * dx[0] + SOFTEN))
                    root = lax.rsqrt(squared)
                    inverse = root * root
                    cube = root * inverse
                    pull = (dot[part, half * 128 : half * 128 + 128] * inverse) * cube
                    for k in range(3):
                        acc[k] += pull * dx[k]
                    first = cube.astype(BF16)
                    highs.append(first)
                    lows.append((cube - first.astype(F32)).astype(BF16))
                for k in range(3):
                    pull_ref[place, k, part, :] = acc[k]
                high.append(jnp.concatenate(highs, axis=1))
                low.append(jnp.concatenate(lows, axis=1))
            sums += lax.dot_general(sum_ref[:, cols], jnp.concatenate(high + low, axis=0), NT, preferred_element_type=F32)
        return sums

    def add_up(tile, place, height, slot, sums):
        sums = sums[:, :height] + sums[:, height:]
        sums = sums[0:8] + sums[8:16] + sums[16:24]
        pulls = [jnp.sum(pull_ref[place, k, :height, :].T, axis=0, keepdims=True) for k in range(3)]
        pulls = jnp.concatenate([jnp.zeros((4, height), F32), *pulls, jnp.zeros((1, height), F32)], axis=0)
        res_ref[tile, :, :height] = sums - slot[:, :height] * sums[3:4] - pulls

    def run(first, heights):
        laid = [lay_out(first + place, place, height) for place, height in enumerate(heights)]
        sums = [add_pairs(place, height, laid[place][1]) for place, height in enumerate(heights)]
        for place, height in enumerate(heights):
            add_up(first + place, place, height, laid[place][0], sums[place])

    halves = (total + HALF - 1) // HALF

    def two_tiles(step, carry):
        run(2 * step, (TILE, TILE))
        return carry

    lax.fori_loop(0, halves >> 2, two_tiles, 0)
    after = (halves >> 2) * 2

    @pl.when((halves & 2) != 0)
    def _():
        run(after, (TILE,))

    @pl.when((halves & 1) != 0)
    def _():
        run(halves >> 1, (HALF,))

    def spread(part, carry):
        first = offset_smem[part]
        tile, start = first >> 7, first & 127
        back = (128 - start) & 127
        moved = jnp.where(lane < 128 - start, pltpu.roll(res_ref[tile], back, 1), pltpu.roll(res_ref[tile + 1], back, 1))
        moved = jnp.where(lane[0:4] < slots, moved[0:4], pltpu.roll(moved[4:8], slots, 1))
        for k in range(3):
            send_ref[part, :, 128 * k : 128 * k + 128] = moved[k : k + 1]
        return carry

    lax.fori_loop(0, parts, spread, 0, unroll=32)


def finish_kernel(count_ref, recv_ref, accel_ref, jerk_ref):
    slots = accel_ref.shape[1]
    total = jnp.sum(recv_ref[...], axis=0)
    for k in range(3):
        row = total[:, 128 * k : 128 * k + 128]
        lane = lax.broadcasted_iota(jnp.int32, row.shape, 1)
        row = jnp.where(lane % slots < count_ref[...], row, 0.0)
        accel_ref[k : k + 1, :] = row[:, :slots]
        jerk_ref[k : k + 1, :] = row[:, slots : 2 * slots]


def pair_call(parts, slots, width):
    tiles = (parts * slots) // TILE + 2
    return pl.pallas_call(
        functools.partial(pair_kernel, slots),
        out_shape=jax.ShapeDtypeStruct((parts, 1, 384), F32),
        in_specs=[vmem()] * 4,
        out_specs=vmem(),
        scratch_shapes=[
            pltpu.SMEM((parts, 128), F32),
            pltpu.SMEM((parts,), jnp.int32),
            pltpu.VMEM((DEPTH, width), BF16),
            pltpu.VMEM((24, width), BF16),
            pltpu.VMEM((tiles, 8, 128), F32),
            pltpu.VMEM((2, 3, TILE, 128), F32),
            pltpu.VMEM((2, 3, TILE, 128), F32),
            pltpu.VMEM((tiles, 8, 128), F32),
            pltpu.SemaphoreType.DMA,
        ],
        compiler_params=pltpu.CompilerParams(vmem_limit_bytes=48 * 1024 * 1024),
    )


def body(parts, positions, velocities, masses, active_index, active_count):
    slots = active_index.shape[0]
    width = positions.shape[1]
    send = pl.pallas_call(
        functools.partial(prepare_kernel, parts),
        out_shape=jax.ShapeDtypeStruct((parts, 1, 384), F32),
        in_specs=[hbm(), vmem(), hbm(), hbm()],
        out_specs=vmem(),
        scratch_shapes=[
            pltpu.SMEM((slots,), jnp.int32),
            pltpu.VMEM((3, width), F32),
            pltpu.VMEM((3, width), F32),
            pltpu.SemaphoreType.DMA((3,)),
        ],
        compiler_params=pltpu.CompilerParams(vmem_limit_bytes=16 * 1024 * 1024),
    )(
        pltpu.with_memory_space_constraint(active_index, pltpu.HBM),
        active_count.reshape(1, 1),
        pltpu.with_memory_space_constraint(positions, pltpu.HBM),
        pltpu.with_memory_space_constraint(velocities, pltpu.HBM),
    )
    received = lax.all_to_all(send, AXES, 0, 0, tiled=True)
    partial_sums = pair_call(parts, slots, width)(received, positions, velocities, masses.reshape(1, width))
    returned = lax.all_to_all(partial_sums, AXES, 0, 0, tiled=True)
    return pl.pallas_call(
        finish_kernel,
        out_shape=(
            jax.ShapeDtypeStruct((3, slots), F32),
            jax.ShapeDtypeStruct((3, slots), F32),
        ),
        in_specs=[vmem(), vmem()],
        out_specs=(vmem(), vmem()),
        compiler_params=pltpu.CompilerParams(vmem_limit_bytes=16 * 1024 * 1024),
    )(active_count.reshape(1, 1), returned)


def solution(mesh):
    parts = int(np.prod([mesh.shape[axis] for axis in AXES]))
    return jax.shard_map(
        functools.partial(body, parts),
        mesh=mesh,
        in_specs=(P(None, AXES), P(None, AXES), P(AXES), P(AXES), P(AXES)),
        out_specs=(P(None, AXES), P(None, AXES)),
        check_vma=False,
    )
```

profile of v0, /device:TPU:0, one launch (start us, length us, event | category | flops | bytes accessed | tf_op | source)
XLA Modules:
  0.0 41.4 jit_solution(10815262008964441205)
XLA Ops:
  1.3 0.0 copy-start.1
  1.3 1.2 %shard_map.68 = f32[32,1,384]{2,1,0:T(1,128)S(1)} custom-call(s32[64]{0:T(128)} %index_hbm.1, s32[1,1]{1,0:T(1,128)} %bitcast.2.count_ref, f32[3,4096]{1,0:T(4,128)} %pos_ref.1, f32[3,4096]{1,0:T(4,128)} %vel_ref.1), custom_call_target="tpu_custom_call" | custom-call | tf_op jit(solution)/shard_map/pallas_call | solution.py:239
  2.5 0.0 copy-start
  2.5 0.0 copy-start.2
  2.6 14.4 %all_to_all.10.recv_ref = f32[32,1,384]{2,1,0:T(1,128)S(1)} all-to-all(f32[32,1,384]{2,1,0:T(1,128)S(1)} %shard_map.68), channel_id=1, replica_groups=mesh['col'=8,'row'=4] {'col','row'}, dimensions={0} | all-to-all | bytes 98304 | tf_op jit(solution)/shard_map/all_to_all | solution.py:257
  17.0 0.0 copy-done.1
  17.0 0.0 copy-done
  17.0 0.0 copy-done.2
  17.0 14.6 %shard_map.69 = f32[32,1,384]{2,1,0:T(1,128)S(1)} custom-call(f32[32,1,384]{2,1,0:T(1,128)S(1)} %all_to_all.10.recv_ref, f32[3,4096]{1,0:T(4,128)S(1)} %copy-done, f32[3,4096]{1,0:T(4,128)S(1)} %copy-done.1, f32[1,4096]{1,0:T(1,128)S(1)} %bitcast.4), custom_call_target="tpu_custom_call" | custom-call | tf_op jit(solution)/shard_map/pallas_call | solution.py:258
  31.6 9.0 %all_to_all.11.recv_ref = f32[32,1,384]{2,1,0:T(1,128)S(1)} all-to-all(f32[32,1,384]{2,1,0:T(1,128)S(1)} %shard_map.69), channel_id=1, replica_groups=mesh['col'=8,'row'=4] {'col','row'}, dimensions={0} | all-to-all | bytes 98304 | tf_op jit(solution)/shard_map/all_to_all | solution.py:259
  40.6 0.7 %shard_map.70 = (f32[3,64]{1,0:T(4,128)}, f32[3,64]{1,0:T(4,128)}) custom-call(s32[1,1]{1,0:T(1,128)} %bitcast.3.count_ref, f32[32,1,384]{2,1,0:T(1,128)S(1)} %all_to_all.11.recv_ref), custom_call_target="tpu_custom_call" | custom-call | tf_op jit(solution)/shard_map/pallas_call | solution.py:260
Async XLA Ops:
  1.3 15.7 %copy-start.1 = (f32[3,4096]{1,0:T(4,128)S(1)}, f32[3,4096]{1,0:T(4,128)}, u32[]{:S(2)}) copy-start(f32[3,4096]{1,0:T(4,128)} %vel_ref.1) | copy-start | bytes 147460
  2.5 14.5 %copy-start = (f32[3,4096]{1,0:T(4,128)S(1)}, f32[3,4096]{1,0:T(4,128)}, u32[]{:S(2)}) copy-start(f32[3,4096]{1,0:T(4,128)} %pos_ref.1) | copy-start | bytes 147460
  2.5 14.5 %copy-start.2 = (f32[4096]{0:T(1024)S(1)}, f32[4096]{0:T(1024)}, u32[]{:S(2)}) copy-start(f32[4096]{0:T(1024)} %param.7) | copy-start | bytes 49156
where the time goes:
time: 41.2 us; the launch traced here: 41.4 us
  blocking collectives  23.5 us (57%)
  Pallas kernels  16.6 us (40%)
  between operations  1.32 us (3%)
    pallas_call x1, Pallas kernels, body(): pair_call(parts, slots, width)  14.6 us
    all_to_all x1, blocking collectives, body(): received = lax.all_to_all(send, AXES, 0, 0, tiled=True)  14.4 us
    all_to_all x1, blocking collectives, body(): returned = lax.all_to_all(partial_sums, AXES, 0, 0, tiled=True)  9.03 us
    pallas_call x1, Pallas kernels, body(): pl.pallas_call(functools.partial(prepare_kernel, parts), out_shape=jax.Sh...  1.24 us

commit v1 on v0

--- a/solution.py
+++ b/solution.py
@@ -87,13 +87,12 @@
         dots = pieces(jnp.concatenate([-heavy * vel, heavy, -heavy * pos, heavy * cross], axis=0))
         for k, (mine, _) in enumerate(PAIRS):
             dot_ref[8 * k : 8 * k + 8, cols] = dots[mine].astype(BF16)
-        dot_ref[RAW:DEPTH, cols] = jnp.zeros((DEPTH - RAW, 512), BF16)
         sums = pieces(jnp.concatenate([mass * pos, mass, mass * vel, jnp.zeros_like(mass)], axis=0))
         for k in range(3):
             sum_ref[8 * k : 8 * k + 8, cols] = sums[k].astype(BF16)
         return carry
 
-    lax.fori_loop(0, width // 512, star_step, 0, unroll=4)
+    lax.fori_loop(0, width // 512, star_step, 0, unroll=8)
     copy.wait()
 
     lane = lax.broadcasted_iota(jnp.int32, (8, 128), 1)
@@ -123,13 +122,13 @@
         for k in range(3):
             own_ref[place, k, :height, :] = jnp.broadcast_to(act[:, RAW + k : RAW + k + 1], (height, 128))
             pull_ref[place, k, :height, :] = jnp.zeros((height, 128), F32)
-        return slot, act.astype(BF16)
+        return slot, act[:, :RAW].astype(BF16)
 
     def add_pairs(place, height, left):
         sums = jnp.zeros((24, 2 * height), F32)
         for block in range(width // BLOCK):
             cols = slice(block * BLOCK, block * BLOCK + BLOCK)
-            dot = lax.dot_general(left, dot_ref[:, cols], NN, preferred_element_type=F32)
+            dot = lax.dot_general(left, dot_ref[:RAW, cols], NN, preferred_element_type=F32)
             high, low = [], []
             for chunk in range(height // CH):
                 part = slice(chunk * CH, chunk * CH + CH)
@@ -221,7 +220,7 @@
         scratch_shapes=[
             pltpu.SMEM((parts, 128), F32),
             pltpu.SMEM((parts,), jnp.int32),
-            pltpu.VMEM((DEPTH, width), BF16),
+            pltpu.VMEM((RAW, width), BF16),
             pltpu.VMEM((24, width), BF16),
             pltpu.VMEM((tiles, 8, 128), F32),
             pltpu.VMEM((2, 3, TILE, 128), F32),

time: 41.2 us -> 41.8 us (1.015); the launches traced: 41.4 us -> 42.6 us
  Pallas kernels: 16.6 us -> 17.8 us
    pallas_call x1, Pallas kernels: 14.6 us -> 15.8 us  [body(): pair_call(parts, slots, width)]
where the time goes in v1:
time: 41.8 us; the launch traced here: 42.6 us
  blocking collectives  23.5 us (56%)
  Pallas kernels  17.8 us (43%)
  between operations  1.32 us (3%)
    pallas_call x1, Pallas kernels, body(): pair_call(parts, slots, width)  15.8 us
    all_to_all x1, blocking collectives, body(): received = lax.all_to_all(send, AXES, 0, 0, tiled=True)  14.4 us
    all_to_all x1, blocking collectives, body(): returned = lax.all_to_all(partial_sums, AXES, 0, 0, tiled=True)  9.03 us
    pallas_call x1, Pallas kernels, body(): pl.pallas_call(functools.partial(prepare_kernel, parts), out_shape=jax.Sh...  1.24 us

profile of v1, /device:TPU:0, one launch (start us, length us, event | category | flops | bytes accessed | tf_op | source)
XLA Modules:
  0.0 42.6 jit_solution(9137528225841137580)
XLA Ops:
  1.3 0.0 copy-start.1
  1.3 1.2 %shard_map.68 = f32[32,1,384]{2,1,0:T(1,128)S(1)} custom-call(s32[64]{0:T(128)} %index_hbm.1, s32[1,1]{1,0:T(1,128)} %bitcast.2.count_ref, f32[3,4096]{1,0:T(4,128)} %pos_ref.1, f32[3,4096]{1,0:T(4,128)} %vel_ref.1), custom_call_target="tpu_custom_call" | custom-call | tf_op jit(solution)/shard_map/pallas_call | solution.py:238
  2.5 0.0 copy-start
  2.5 0.0 copy-start.2
  2.6 14.4 %all_to_all.10.recv_ref = f32[32,1,384]{2,1,0:T(1,128)S(1)} all-to-all(f32[32,1,384]{2,1,0:T(1,128)S(1)} %shard_map.68), channel_id=1, replica_groups=mesh['col'=8,'row'=4] {'col','row'}, dimensions={0} | all-to-all | bytes 98304 | tf_op jit(solution)/shard_map/all_to_all | solution.py:256
  17.0 0.0 copy-done.1
  17.0 0.0 copy-done
  17.0 0.0 copy-done.2
  17.0 15.8 %shard_map.69 = f32[32,1,384]{2,1,0:T(1,128)S(1)} custom-call(f32[32,1,384]{2,1,0:T(1,128)S(1)} %all_to_all.10.recv_ref, f32[3,4096]{1,0:T(4,128)S(1)} %copy-done, f32[3,4096]{1,0:T(4,128)S(1)} %copy-done.1, f32[1,4096]{1,0:T(1,128)S(1)} %bitcast.4), custom_call_target="tpu_custom_call" | custom-call | tf_op jit(solution)/shard_map/pallas_call | solution.py:257
  32.8 9.0 %all_to_all.11.recv_ref = f32[32,1,384]{2,1,0:T(1,128)S(1)} all-to-all(f32[32,1,384]{2,1,0:T(1,128)S(1)} %shard_map.69), channel_id=1, replica_groups=mesh['col'=8,'row'=4] {'col','row'}, dimensions={0} | all-to-all | bytes 98304 | tf_op jit(solution)/shard_map/all_to_all | solution.py:258
  41.9 0.7 %shard_map.70 = (f32[3,64]{1,0:T(4,128)}, f32[3,64]{1,0:T(4,128)}) custom-call(s32[1,1]{1,0:T(1,128)} %bitcast.3.count_ref, f32[32,1,384]{2,1,0:T(1,128)S(1)} %all_to_all.11.recv_ref), custom_call_target="tpu_custom_call" | custom-call | tf_op jit(solution)/shard_map/pallas_call | solution.py:259
Async XLA Ops:
  1.3 15.7 %copy-start.1 = (f32[3,4096]{1,0:T(4,128)S(1)}, f32[3,4096]{1,0:T(4,128)}, u32[]{:S(2)}) copy-start(f32[3,4096]{1,0:T(4,128)} %vel_ref.1) | copy-start | bytes 147460
  2.5 14.5 %copy-start = (f32[3,4096]{1,0:T(4,128)S(1)}, f32[3,4096]{1,0:T(4,128)}, u32[]{:S(2)}) copy-start(f32[3,4096]{1,0:T(4,128)} %pos_ref.1) | copy-start | bytes 147460
  2.5 14.5 %copy-start.2 = (f32[4096]{0:T(1024)S(1)}, f32[4096]{0:T(1024)}, u32[]{:S(2)}) copy-start(f32[4096]{0:T(1024)} %param.7) | copy-start | bytes 49156
